TPU v7x, 512 devices: a whole 4x4x16 slice. The times are simulated.
512 devices in a mesh: rows: 128 (over x, z_lo, y), feat: 4 (over z_hi, core).
Axes of the slice: x: 4, y: 4, z: 16 (z_hi: 2, z_lo: 8; z = z_hi * 8 + z_lo), core: 2. Of those that a mesh axis runs over, the one named last changes fastest.
Arguments:
- features: bfloat16 [32768, 512], P('rows', 'feat'), may hold values from -6 to 6
- weight: bfloat16 [512, 512], P(None, 'feat'), may hold values from -0.25 to 0.25
- block_values: bfloat16 [256, 8, 128, 128], P('rows', 'feat'), may hold values from -0.25 to 0.25
- columns: int32 [256, 8], P('rows'), may hold values from 0 to 255, as said below
- counts: int32 [256], P('rows'), may hold values from 2 to 8, as said below
- cotangent: bfloat16 [32768, 512], P('rows', 'feat'), may hold values from -6 to 6
Outputs:
- hidden: bfloat16 [32768, 512], P('rows', 'feat')
- grad_features: bfloat16 [32768, 512], P('rows', 'feat')
- grad_weight: float32 [512, 512], P(None, 'feat')
Inputs may be any that keep to these rules, and one draw needn't show every extreme that they name: `columns`: the 8 column blocks of a row block are distinct and lie on the devices within 4 indices of the row block's own index along rows, counted around the axis (the device of block c is c // 2). Slots 0 to counts[g] - 1 of row block g are live, the others are ignored; some row block has exactly 8 live slots.
All inputs are finite; a program needn't handle non-finite values.
Results may differ from a plain program's by a relative error of at most 0.0067.
Values may be sent and summed in bfloat16 or wider, within the bound.
No kernel may reach another device: no remote copies, remote signals or barrier semaphores. Data moves between devices by JAX's collectives and lax.ppermute only.
A program may use at most 64 MiB of HBM per device.

v0:
```python
import jax
import jax.numpy as jnp
from jax import lax
from jax.sharding import PartitionSpec as P


def shifted(value, axis, steps):
    count = lax.axis_size(axis)
    pairs = [(source, (source + steps) % count) for source in range(count)]
    return lax.ppermute(value, axis, pairs)


def activation(values):
    return jax.nn.gelu(values, approximate=True)


def window_index(columns, row_blocks, center, halo_reach, row_count):
    owner_dev = columns // row_blocks
    offset = (owner_dev - center + halo_reach + row_count) % row_count
    return offset * row_blocks + columns % row_blocks


def live_tiles(panel_part, first_slot, counts, places):
    slot_count = panel_part.shape[1]
    slot_ids = first_slot + jnp.arange(slot_count)
    slot_live = counts[:, None] > slot_ids[None, :]
    tiles = jnp.where(slot_live[:, :, None, None], panel_part, jnp.zeros((), panel_part.dtype))
    return (tiles, places)


def gather_slots(panel_part, first_slot, counts, places, window):
    tiles, targets = live_tiles(panel_part, first_slot, counts, places)
    picked = jnp.take(window, targets, axis=0)
    product = jnp.einsum("gsij,gsjf->gif", tiles, picked, preferred_element_type=jnp.float32)
    return product


def spread_slots(running, panel_part, first_slot, counts, places, grad_blocks):
    tiles, targets = live_tiles(panel_part, first_slot, counts, places)
    block_size = grad_blocks.shape[1]
    feat_width = grad_blocks.shape[2]
    product = jnp.einsum("gsij,gif->gsjf", tiles, grad_blocks, preferred_element_type=jnp.float32)
    return running.at[targets.reshape(-1)].add(product.reshape(-1, block_size, feat_width))


def on_device(features, weight, block_values, columns, counts, cotangent):
    row_count = lax.axis_size("rows")
    center = lax.axis_index("rows")
    halo_reach = min(4, (row_count - 1) // 3)
    row_blocks = counts.shape[0]
    block_size = block_values.shape[2]
    feat_width = features.shape[1]
    local_rows = features.shape[0]
    span_blocks = (2 * halo_reach + 1) * row_blocks
    pieces = {0: features}
    for offset in list(range(-halo_reach, 0)) + list(range(1, halo_reach + 1)):
        pieces[offset] = shifted(features, "rows", -offset)
    window = jnp.stack([pieces[offset] for offset in range(-halo_reach, halo_reach + 1)])
    window = window.reshape(span_blocks, block_size, feat_width)
    places = window_index(columns, row_blocks, center, halo_reach, row_count)
    panel_full = lax.all_gather(block_values, "feat", axis=1, tiled=True)
    summed = gather_slots(panel_full, 0, counts, places, window)
    aggregated = summed.reshape(local_rows, feat_width).astype(jnp.bfloat16)
    agg_full, weight_full = (
        lax.all_gather(aggregated, "feat", axis=1, tiled=True),
        lax.all_gather(weight, "feat", axis=1, tiled=True),
    )
    pre_act = jnp.dot(agg_full, weight, preferred_element_type=jnp.float32)
    hidden, act_grad = jax.vjp(activation, pre_act)
    grad_pre = act_grad(cotangent.astype(jnp.float32))[0].astype(jnp.bfloat16)
    grad_full = lax.all_gather(grad_pre, "feat", axis=1, tiled=True)
    weight_terms = lax.dot_general(
        agg_full, grad_pre, (((0,), (0,)), ((), ())), preferred_element_type=jnp.float32
    )
    node_total = local_rows * row_count
    grad_weight = lax.psum(weight_terms, "rows") * float(node_total) ** (-0.5)
    feat_index = lax.axis_index("feat")
    weight_rows = lax.dynamic_slice_in_dim(weight_full, feat_index * feat_width, feat_width, 0)
    grad_agg = lax.dot_general(
        grad_full, weight_rows, (((1,), (1,)), ((), ())), preferred_element_type=jnp.float32
    )
    grad_blocks = grad_agg.astype(jnp.bfloat16).reshape(row_blocks, block_size, feat_width)
    zero_window = jnp.zeros((span_blocks, block_size, feat_width), jnp.float32)
    spread = spread_slots(zero_window, panel_full, 0, counts, places, grad_blocks)
    spread = spread.reshape(2 * halo_reach + 1, local_rows, feat_width)
    grad_local = spread[halo_reach]
    for offset in list(range(-halo_reach, 0)) + list(range(1, halo_reach + 1)):
        outgoing = spread[halo_reach + offset].astype(jnp.bfloat16)
        arrived = shifted(outgoing, "rows", offset)
        grad_local = grad_local + arrived.astype(jnp.float32)
    return (hidden.astype(jnp.bfloat16), grad_local.astype(jnp.bfloat16), grad_weight)


def solution(mesh):
    in_specs = (
        P("rows", "feat"),
        P(None, "feat"),
        P("rows", "feat", None, None),
        P("rows", None),
        P("rows"),
        P("rows", "feat"),
    )
    out_specs = (P("rows", "feat"), P("rows", "feat"), P(None, "feat"))
    return jax.shard_map(
        on_device, mesh=mesh, in_specs=in_specs, out_specs=out_specs, check_vma=False
    )
```

profile of v0, /device:TPU:0, one launch (start us, length us, event | category | flops | bytes accessed | tf_op | source)
XLA Modules:
  0.0 2029.0 jit_solution(9673792675788454822)
XLA Ops:
  7.2 12.6 collective-permute-start.5
  19.9 3.0 collective-permute-start.4
  22.8 2.9 collective-permute-start.3
  25.7 2.6 collective-permute-start.2
  28.4 1.9 collective-permute-start
  31.9 20.9 %all_gather.12 = bf16[2,8,128,128]{3,2,1,0:T(8,128)(2,1)S(1)} all-gather(bf16[2,2,128,128]{3,2,1,0:T(8,128)(2,1)} %param.8), channel_id=1, replica_groups=mesh['rows'=128,'feat'=4] {'feat'}, dimensions={1}, use_global_device_ids=true | all-gather | bytes 655360 | tf_op jit(solution)/shard_map/all_gather | solution.py:61
  52.8 20.9 %all_gather.15 = bf16[512,512]{1,0:T(8,128)(2,1)S(1)} all-gather(bf16[512,128]{1,0:T(8,128)(2,1)} %param.7), channel_id=1, replica_groups=mesh['rows'=128,'feat'=4] {'feat'}, dimensions={1}, use_global_device_ids=true | all-gather | bytes 655360 | tf_op jit(solution)/shard_map/all_gather | solution.py:66
  73.7 1.9 collective-permute-start.1
  75.7 14.1 collective-permute-done.1
  89.7 1.9 collective-permute-start.7
  91.7 2.0 collective-permute-start.6
  93.8 5.3 collective-permute-done.6
  100.2 15.2 all_gather.13
  116.3 14.6 all_gather.14
  133.5 3.3 collective-permute-start.15
  136.8 11.3 collective-permute-start.8
  148.1 5.2 collective-permute-start.14
  153.2 3.1 collective-permute-start.13
  156.3 1.9 collective-permute-start.12
  158.2 14.7 collective-permute-start.11
  173.0 3.1 collective-permute-start.10
  176.1 3.9 collective-permute-start.9
  181.0 2.4 collective-permute-done.9
  184.2 1836.3 %all-reduce.2.cloned.1.call-done = f32[512,128]{1,0:T(8,128)} async-done(((f32[512,128]{1,0:T(8,128)}), f32[512,128]{1,0:T(8,128)}) %all-reduce.2.cloned.1.call-update) | async-done | bytes 262160 | tf_op jit(solution)/shard_map/psum | solution.py:76
  (50 shorter events, 9.6 us)
Async XLA Ops:
  7.2 66.6 %copy-start.1 = (bf16[256,128]{1,0:T(8,128)(2,1)S(1)}, bf16[256,128]{1,0:T(8,128)(2,1)}, u32[]{:S(2)}) copy-start(bf16[256,128]{1,0:T(8,128)(2,1)} %param.6) | copy-start | bytes 196612
  7.2 2013.3 %all-reduce.2.cloned.1.call-start = ((), (), s32[]{:S(2)}) async-start(), calls=%async_computation | async-start | bytes 524288 | tf_op jit(solution)/shard_map/psum | solution.py:76
  7.2 86.5 %collective-permute-start.5 = (bf16[256,128]{1,0:T(8,128)(2,1)}, bf16[256,128]{1,0:T(8,128)(2,1)S(1)}, u32[]{:S(2)}, u32[]{:S(2)}) collective-permute-start(bf16[256,128]{1,0:T(8,128)(2,1)} %param.6), channel_id=1, source_target_pairs={{0,504},{4,508},{8,0},{12,4},{16,8},{20,12},{24,16},{28,20},{32,24... | collective-permute-start | bytes 196616 | tf_op jit(solution)/shard_map/ppermute | solution.py:10
  19.9 73.9 %collective-permute-start.4 = (bf16[256,128]{1,0:T(8,128)(2,1)}, bf16[256,128]{1,0:T(8,128)(2,1)S(1)}, u32[]{:S(2)}, u32[]{:S(2)}) collective-permute-start(bf16[256,128]{1,0:T(8,128)(2,1)} %param.6), channel_id=1, source_target_pairs={{0,508},{4,0},{8,4},{12,8},{16,12},{20,16},{24,20},{28,24},{32,28}... | collective-permute-start | bytes 196616 | tf_op jit(solution)/shard_map/ppermute | solution.py:10
  22.8 70.8 %collective-permute-start.3 = (bf16[256,128]{1,0:T(8,128)(2,1)}, bf16[256,128]{1,0:T(8,128)(2,1)S(1)}, u32[]{:S(2)}, u32[]{:S(2)}) collective-permute-start(bf16[256,128]{1,0:T(8,128)(2,1)} %param.6), channel_id=1, source_target_pairs={{0,4},{4,8},{8,12},{12,16},{16,20},{20,24},{24,28},{28,32},{32,36}... | collective-permute-start | bytes 196616 | tf_op jit(solution)/shard_map/ppermute | solution.py:10
  25.7 66.0 %collective-permute-start.2 = (bf16[256,128]{1,0:T(8,128)(2,1)}, bf16[256,128]{1,0:T(8,128)(2,1)S(1)}, u32[]{:S(2)}, u32[]{:S(2)}) collective-permute-start(bf16[256,128]{1,0:T(8,128)(2,1)} %param.6), channel_id=1, source_target_pairs={{0,8},{4,12},{8,16},{12,20},{16,24},{20,28},{24,32},{28,36},{32,40... | collective-permute-start | bytes 196616 | tf_op jit(solution)/shard_map/ppermute | solution.py:10
  28.4 45.4 %collective-permute-start = (bf16[256,128]{1,0:T(8,128)(2,1)}, bf16[256,128]{1,0:T(8,128)(2,1)S(1)}, u32[]{:S(2)}, u32[]{:S(2)}) collective-permute-start(bf16[256,128]{1,0:T(8,128)(2,1)} %param.6), channel_id=1, source_target_pairs={{0,16},{4,20},{8,24},{12,28},{16,32},{20,36},{24,40},{28,44},{32,4... | collective-permute-start | bytes 196616 | tf_op jit(solution)/shard_map/ppermute | solution.py:10
  73.7 16.0 collective-permute-start.1
  89.7 9.3 collective-permute-start.7
  91.7 7.4 collective-permute-start.6
  99.8 15.6 copy-start
  99.8 15.6 copy-start.2
  133.5 24.7 %collective-permute-start.15 = (bf16[256,128]{1,0:T(8,128)(2,1)S(1)}, bf16[256,128]{1,0:T(8,128)(2,1)S(1)}, u32[]{:S(2)}, u32[]{:S(2)}) collective-permute-start(bf16[256,128]{1,0:T(8,128)(2,1)S(1)} %bitcast.77), channel_id=1, source_target_pairs={{0,16},{4,20},{8,24},{12,28},{16,32},{20,36},{24,40},{28,44},{32,4... | collective-permute-start | bytes 196616 | tf_op jit(solution)/shard_map/ppermute | solution.py:10
  136.8 36.2 %collective-permute-start.8 = (bf16[256,128]{1,0:T(8,128)(2,1)S(1)}, bf16[256,128]{1,0:T(8,128)(2,1)S(1)}, u32[]{:S(2)}, u32[]{:S(2)}) collective-permute-start(bf16[256,128]{1,0:T(8,128)(2,1)S(1)} %bitcast.76), channel_id=1, source_target_pairs={{0,496},{4,500},{8,504},{12,508},{16,0},{20,4},{24,8},{28,12},{32,... | collective-permute-start | bytes 196616 | tf_op jit(solution)/shard_map/ppermute | solution.py:10
  148.1 28.0 %collective-permute-start.14 = (bf16[256,128]{1,0:T(8,128)(2,1)S(1)}, bf16[256,128]{1,0:T(8,128)(2,1)S(1)}, u32[]{:S(2)}, u32[]{:S(2)}) collective-permute-start(bf16[256,128]{1,0:T(8,128)(2,1)S(1)} %bitcast.75), channel_id=1, source_target_pairs={{0,12},{4,16},{8,20},{12,24},{16,28},{20,32},{24,36},{28,40},{32,4... | collective-permute-start | bytes 196616 | tf_op jit(solution)/shard_map/ppermute | solution.py:10
  153.2 27.8 %collective-permute-start.13 = (bf16[256,128]{1,0:T(8,128)(2,1)S(1)}, bf16[256,128]{1,0:T(8,128)(2,1)S(1)}, u32[]{:S(2)}, u32[]{:S(2)}) collective-permute-start(bf16[256,128]{1,0:T(8,128)(2,1)S(1)} %bitcast.74), channel_id=1, source_target_pairs={{0,8},{4,12},{8,16},{12,20},{16,24},{20,28},{24,32},{28,36},{32,40... | collective-permute-start | bytes 196616 | tf_op jit(solution)/shard_map/ppermute | solution.py:10
  156.3 24.7 %collective-permute-start.12 = (bf16[256,128]{1,0:T(8,128)(2,1)S(1)}, bf16[256,128]{1,0:T(8,128)(2,1)S(1)}, u32[]{:S(2)}, u32[]{:S(2)}) collective-permute-start(bf16[256,128]{1,0:T(8,128)(2,1)S(1)} %bitcast.73), channel_id=1, source_target_pairs={{0,4},{4,8},{8,12},{12,16},{16,20},{20,24},{24,28},{28,32},{32,36}... | collective-permute-start | bytes 196616 | tf_op jit(solution)/shard_map/ppermute | solution.py:10
  158.2 22.8 %collective-permute-start.11 = (bf16[256,128]{1,0:T(8,128)(2,1)S(1)}, bf16[256,128]{1,0:T(8,128)(2,1)S(1)}, u32[]{:S(2)}, u32[]{:S(2)}) collective-permute-start(bf16[256,128]{1,0:T(8,128)(2,1)S(1)} %bitcast.72), channel_id=1, source_target_pairs={{0,508},{4,0},{8,4},{12,8},{16,12},{20,16},{24,20},{28,24},{32,28}... | collective-permute-start | bytes 196616 | tf_op jit(solution)/shard_map/ppermute | solution.py:10
  173.0 8.0 collective-permute-start.10
  176.1 7.4 collective-permute-start.9
Sparse Core Ops, SparseCore 0:
  181.1 1839.3 all-reduce.1
where the time goes:
time: 2030 us
  waiting for transfers between devices  1860 us (92%)
  starting transfers between devices  75.2 us (4%)
  blocking collectives  71.7 us (4%)
    psum x1, waiting for transfers between devices, on_device(): grad_weight = lax.psum(weight_terms, 'rows') * float(node_total) ** (-0.5)  1840 us
    ppermute x16, starting transfers between devices, shifted(): return lax.ppermute(value, axis, pairs)  75.2 us
  transfers between devices with their start and end apart: 17, of which 4 were waited for; matrix products, arithmetic and copies ran while one was open for 0% of the time, Pallas kernels for 0%

commit v1 on v0

v1 whole, which is shorter than its diff:
```python
import functools

import jax
import jax.numpy as jnp
from jax import lax
from jax.experimental import pallas as pl
from jax.experimental.pallas import tpu as pltpu
from jax.sharding import PartitionSpec as P

X, ZL, Y = 4, 8, 4
R = X * ZL * Y
FB = 128
RB = 2
REACH = 4
S = 8
GY = [[x * 32 + z * 4 + y for y in range(Y)] for x in range(X) for z in range(ZL)]
GZ = [[x * 32 + z * 4 + y for z in range(ZL)] for x in range(X) for y in range(Y)]
GXY = [[x * 32 + z * 4 + y for x in range(X) for y in range(Y)] for z in range(ZL)]
SWAP_A = [(r, (r + 4) % R if (r // 4) % 2 == 0 else (r - 4) % R) for r in range(R)]
SWAP_B = [(r, (r - 4) % R if (r // 4) % 2 == 0 else (r + 4) % R) for r in range(R)]
CROSS = [(f, f ^ 2) for f in range(4)]
SIBLING = [(f, f ^ 1) for f in range(4)]
FLIPS = (0, 2, 1, 3)
F32 = jnp.float32
BF16 = jnp.bfloat16


def window_place(col, r):
    y = r & 3
    off = ((col >> 1) - r + REACH + R) & (R - 1)
    t = y + off
    s = t & 3
    dq = (t >> 2) - 1
    piece = jnp.where(dq == 0, s * 2, jnp.where((dq == 1) & (s == y), 8, s * 2 + 1))
    return jnp.clip(piece * 2 + (col & 1), 0, 17)


def slot_of(p, j, f):
    return (f ^ FLIPS[p]) * 2 + j


def gather_kernel(ids, columns, counts, own, cross, pair, win, last, agg):
    r, f = ids[0], ids[1]
    for g in range(RB):
        total = jnp.zeros((FB, FB), F32)
        for p in range(4):
            for j in range(2):
                slot = slot_of(p, j, f)
                place = window_place(columns[g, slot], r)
                base = (g * 2 + j) * FB
                if p == 0:
                    tile = own[base : base + FB, :]
                elif p == 1:
                    tile = cross[base : base + FB, :]
                else:
                    start = (p - 2) * 1280 + base
                    tile = pair[start : start + FB, :]
                live = counts[g] > slot
                tile = jnp.where(live, tile, jnp.zeros_like(tile))
                block = win[place]
                total = total + jnp.dot(tile, block, preferred_element_type=F32)
        agg[g * FB : (g + 1) * FB, :] = total.astype(BF16)


def main_kernel(ids, columns, counts, own, cross, pair, agg, hidden, terms, mine, send, send_last, wnd, grad):
    r, f = ids[0], ids[1]
    y = r & 3
    k0 = 0.7978845608028654
    wide = jnp.concatenate([agg[k] for k in range(4)], axis=1)
    grad_agg = jnp.zeros((RB * FB, FB), F32)
    for p in range(4):
        ref, start = ((own, 0), (cross, 0), (pair, 0), (pair, 1280))[p]
        weight = ref[start + 768 : start + 1280, :]
        cot = ref[start + 512 : start + 768, :].astype(F32)
        v = jnp.dot(wide, weight, preferred_element_type=F32)
        v2 = v * v
        t = jnp.tanh(k0 * (v + 0.044715 * (v * v2)))
        half = 0.5 * (1.0 + t)
        if p == 0:
            hidden[...] = (v * half).astype(BF16)
        slope = half + 0.5 * v * (1.0 - t * t) * (k0 * (1.0 + 3 * 0.044715 * v2))
        grad_pre = (cot * slope).astype(BF16)
        if p == 0:
            terms[...] = lax.dot_general(
                wide, grad_pre, (((0,), (0,)), ((), ())), preferred_element_type=F32
            ).astype(BF16)
        rows = ref[pl.ds(pl.multiple_of(start + 768 + f * FB, FB), FB), :]
        grad_agg = grad_agg + lax.dot_general(
            grad_pre, rows, (((1,), (1,)), ((), ())), preferred_element_type=F32
        )
    grad[...] = grad_agg.astype(BF16)
    for b in range(18):
        wnd[b] = jnp.zeros((FB, FB), F32)
    for g in range(RB):
        part = grad[g * FB : (g + 1) * FB, :]
        for p in range(4):
            for j in range(2):
                slot = slot_of(p, j, f)
                place = window_place(columns[g, slot], r)
                ref, start = ((own, 0), (cross, 0), (pair, 0), (pair, 1280))[p]
                base = start + (g * 2 + j) * FB
                tile = ref[base : base + FB, :]
                live = counts[g] > slot
                tile = jnp.where(live, tile, jnp.zeros_like(tile))
                product = lax.dot_general(
                    tile, part, (((0,), (0,)), ((), ())), preferred_element_type=F32
                )
                wnd[place] = wnd[place] + product
    for b in range(16):
        send[b] = wnd[b].astype(BF16)
    for b in range(2):
        send_last[b] = wnd[16 + b]
        mine[b] = wnd[y * 4 + b]


def call(kernel, out_shape, scratch, *args):
    smem = pl.BlockSpec(memory_space=pltpu.SMEM)
    vmem = pl.BlockSpec(memory_space=pltpu.VMEM)
    return pl.pallas_call(
        kernel,
        out_shape=out_shape,
        in_specs=[smem] * 3 + [vmem] * (len(args) - 3),
        out_specs=jax.tree.map(lambda _: vmem, out_shape),
        scratch_shapes=scratch,
    )(*args)


def on_device(features, weight, block_values, columns, counts, cotangent):
    r = lax.axis_index("rows")
    f = lax.axis_index("feat")
    y = r % 4
    even = (r // 4) % 2 == 0
    ids = jnp.stack([r, f]).astype(jnp.int32)
    rows = features.shape[0]

    own = jnp.concatenate([block_values.reshape(4 * FB, FB), cotangent, weight], axis=0)
    cross = lax.ppermute(own, "feat", CROSS)
    from_b = lax.ppermute(features, "rows", SWAP_B)
    from_a = lax.ppermute(features, "rows", SWAP_A)
    nxt = jnp.where(even, from_a, from_b)
    prv = jnp.where(even, from_b, from_a)
    dest = jnp.arange(4)[:, None, None]
    extra = jnp.where(dest > y, nxt[None], prv[None])
    outgoing = jnp.stack([jnp.broadcast_to(features[None], (4, rows, FB)), extra], axis=1)
    arrived = lax.all_to_all(outgoing, "rows", 0, 0, axis_index_groups=GY, tiled=True)
    window = jnp.concatenate([arrived.reshape(16, FB, FB), nxt.reshape(2, FB, FB)], axis=0)
    pair = lax.ppermute(jnp.concatenate([own, cross], axis=0), "feat", SIBLING)

    agg = call(
        gather_kernel,
        jax.ShapeDtypeStruct((rows, FB), BF16),
        [],
        ids, columns, counts, own, cross, pair, window, nxt,
    )
    agg_full = lax.all_gather(agg, "feat", axis=0, tiled=False)
    hidden, terms, mine, send, send_last = call(
        main_kernel,
        (
            jax.ShapeDtypeStruct((rows, FB), BF16),
            jax.ShapeDtypeStruct((4 * FB, FB), BF16),
            jax.ShapeDtypeStruct((2, FB, FB), F32),
            jax.ShapeDtypeStruct((16, FB, FB), BF16),
            jax.ShapeDtypeStruct((2, FB, FB), F32),
        ),
        [pltpu.VMEM((18, FB, FB), F32), pltpu.VMEM((rows, FB), BF16)],
        ids, columns, counts, own, cross, pair, agg_full,
    )

    got = lax.all_to_all(
        send.reshape(4, 2, rows, FB), "rows", 0, 0, axis_index_groups=GY, tiled=True
    ).astype(F32)
    source = jnp.arange(4)[:, None, None]
    here = mine.reshape(rows, FB) + jnp.where(source == y, 0.0, got[:, 0]).sum(0)
    to_prv = jnp.where(source <= y, got[:, 1], 0.0).sum(0)
    to_nxt = jnp.where(source > y, got[:, 1], 0.0).sum(0) + send_last.reshape(rows, FB)
    to_prv, to_nxt = to_prv.astype(BF16), to_nxt.astype(BF16)
    back_b = lax.ppermute(jnp.where(even, to_prv, to_nxt), "rows", SWAP_B)
    back_a = lax.ppermute(jnp.where(even, to_nxt, to_prv), "rows", SWAP_A)
    grad_features = (here + back_a.astype(F32) + back_b.astype(F32)).astype(BF16)

    parts = lax.all_to_all(terms.reshape(16, 32, FB), "rows", 0, 0, axis_index_groups=GXY, tiled=True)
    part = parts.astype(F32).sum(0)
    layers = lax.all_to_all(
        jnp.broadcast_to(part[None], (8, 32, FB)), "rows", 0, 0, axis_index_groups=GZ, tiled=True
    )
    total = (layers.sum(0) * float(rows * R) ** (-0.5)).astype(BF16)
    grad_weight = lax.all_to_all(
        jnp.broadcast_to(total[None], (16, 32, FB)), "rows", 0, 0, axis_index_groups=GXY, tiled=True
    )
    return hidden, grad_features, grad_weight.reshape(4 * FB, FB).astype(F32)


def solution(mesh):
    in_specs = (
        P("rows", "feat"),
        P(None, "feat"),
        P("rows", "feat", None, None),
        P("rows", None),
        P("rows"),
        P("rows", "feat"),
    )
    out_specs = (P("rows", "feat"), P("rows", "feat"), P(None, "feat"))
    return jax.shard_map(
        on_device, mesh=mesh, in_specs=in_specs, out_specs=out_specs, check_vma=False
    )
```

time: 2030 us -> 156 us (0.08)
  the two profiles are of different devices: /device:TPU:0 before, /device:TPU:32 now
where the time goes in v1:
time: 156 us; the launch traced here: 155 us
  starting transfers between devices  59.6 us (38%)
  waiting for transfers between devices  53.1 us (34%)
  blocking collectives  26.9 us (17%)
  other arithmetic  6.09 us (4%)
  Pallas kernels  5.91 us (4%)
  local copies, waits for them, and re-layouts  2.96 us (2%)
    ppermute x1, waiting for transfers between devices, on_device(): cross = lax.ppermute(own, 'feat', CROSS)  27.6 us
    all_gather x1, blocking collectives, on_device(): agg_full = lax.all_gather(agg, 'feat', axis=0, tiled=False)  15.1 us
    ppermute x1, starting transfers between devices, on_device(): from_a = lax.ppermute(features, 'rows', SWAP_A)  13.5 us
    all_to_all x1, blocking collectives, on_device(): lax.all_to_all(terms.reshape(16, 32, FB), 'rows', 0, 0, axis_index_groups...  11.7 us
    ppermute x1, starting transfers between devices, on_device(): back_a = lax.ppermute(jnp.where(even, to_nxt, to_prv), 'rows', SWAP_A)  9.84 us
    all_to_all x1, waiting for transfers between devices, on_device(): lax.all_to_all(outgoing, 'rows', 0, 0, axis_index_groups=GY, tiled=True)  9.56 us
    all_to_all x1, waiting for transfers between devices, on_device(): lax.all_to_all(send.reshape(4, 2, rows, FB), 'rows', 0, 0, axis_index_gro...  8.82 us
    ppermute x1, starting transfers between devices, on_device(): cross = lax.ppermute(own, 'feat', CROSS)  8.35 us
  transfers between devices with their start and end apart: 10, of which 4 were waited for; matrix products, arithmetic and copies ran while one was open for 3% of the time, Pallas kernels for 0%

profile of v1, /device:TPU:32, one launch (start us, length us, event | category | flops | bytes accessed | tf_op | source)
XLA Modules:
  0.0 155.4 jit_solution(11317695201634754436)
XLA Ops:
  0.7 4.0 %collective-permute-start.3 = (bf16[256,128]{1,0:T(8,128)(2,1)}, bf16[256,128]{1,0:T(8,128)(2,1)S(1)}, u32[]{:S(2)}, u32[]{:S(2)}) collective-permute-start(bf16[256,128]{1,0:T(8,128)(2,1)} %param.6), channel_id=1, source_target_pairs={{0,496},{4,500},{8,504},{12,508},{16,32},{20,36},{24,40},{28,44},{... | collective-permute-start | bytes 196616 | tf_op jit(solution)/shard_map/ppermute | solution.py:138
  4.6 13.5 %collective-permute-start.2 = (bf16[256,128]{1,0:T(8,128)(2,1)}, bf16[256,128]{1,0:T(8,128)(2,1)S(1)}, u32[]{:S(2)}, u32[]{:S(2)}) collective-permute-start(bf16[256,128]{1,0:T(8,128)(2,1)} %param.6), channel_id=1, source_target_pairs={{0,16},{4,20},{8,24},{12,28},{16,0},{20,4},{24,8},{28,12},{32,48},... | collective-permute-start | bytes 196616 | tf_op jit(solution)/shard_map/ppermute | solution.py:139
  18.2 1.0 pad_maximum_fusion.3.own
  19.2 8.4 %collective-permute-start = (bf16[1280,128]{1,0:T(8,128)(2,1)S(1)}, bf16[1280,128]{1,0:T(8,128)(2,1)S(1)}, u32[]{:S(2)}, u32[]{:S(2)}) collective-permute-start(bf16[1280,128]{1,0:T(8,128)(2,1)S(1)} %pad_maximum_fusion.3.own), channel_id=1, source_target_pairs={{0,2},{1,3},{2,0},{3,1},{4,6},{5,7},{6,4},{7,5},{8,10},{9,11},{10,... | collective-permute-start | bytes 983048 | tf_op jit(solution)/shard_map/ppermute | solution.py:137
  27.7 27.6 %collective-permute-done.cross = bf16[1280,128]{1,0:T(8,128)(2,1)S(1)} collective-permute-done((bf16[1280,128]{1,0:T(8,128)(2,1)S(1)}, bf16[1280,128]{1,0:T(8,128)(2,1)S(1)}, u32[]{:S(2)}, u32[]{:S(2)}) %collective-permute-start) | collective-permute-done | bytes 327712 | tf_op jit(solution)/shard_map/ppermute | solution.py:137
  55.3 0.9 pad_maximum_fusion
  56.2 1.9 %collective-permute-start.1 = (bf16[2560,128]{1,0:T(8,128)(2,1)S(1)}, bf16[2560,128]{1,0:T(8,128)(2,1)S(1)}, u32[]{:S(2)}, u32[]{:S(2)}) collective-permute-start(bf16[2560,128]{1,0:T(8,128)(2,1)S(1)} %pad_maximum_fusion), channel_id=1, source_target_pairs={{0,1},{1,0},{2,3},{3,2},{4,5},{5,4},{6,7},{7,6},{8,9},{9,8},{10,11... | collective-permute-start | bytes 1966088 | tf_op jit(solution)/shard_map/ppermute | solution.py:147
  58.3 0.8 pad_maximum_fusion.2
  59.2 4.5 %all-to-all-start = ((bf16[4,2,256,128]{3,2,1,0:T(8,128)(2,1)}), bf16[4,2,256,128]{3,2,1,0:T(8,128)(2,1)S(1)}, u32[]{:S(2)}, u32[]{:S(2)}) async-start(bf16[4,2,256,128]{3,2,1,0:T(8,128)(2,1)} %pad_maximum_fusion.2), calls=%async_computation | async-start | bytes 1048576 | tf_op jit(solution)/shard_map/all_to_all | solution.py:145
  64.2 9.6 %all-to-all-done = bf16[4,2,256,128]{3,2,1,0:T(8,128)(2,1)S(1)} async-done(((bf16[4,2,256,128]{3,2,1,0:T(8,128)(2,1)}), bf16[4,2,256,128]{3,2,1,0:T(8,128)(2,1)S(1)}, u32[]{:S(2)}, u32[]{:S(2)}) %all-to-all-start) | async-done | bytes 524320 | tf_op jit(solution)/shard_map/all_to_all | solution.py:145
  73.8 0.9 pad_maximum_fusion.1.win
  74.7 0.9 copy-done.2
  75.5 2.4 %shard_map.85 = bf16[256,128]{1,0:T(8,128)(2,1)} custom-call(s32[2]{0:T(128)} %pad_add_fusion.ids, s32[2,8]{1,0:T(2,128)} %columns.3, s32[2]{0:T(128)} %counts.3, bf16[1280,128]{1,0:T(8,128)(2,1)} %copy-done.1, bf16[1280,128]{1,0:T(8,128)(2,1)} %copy-done, bf16[2560,128]{1,0:T(8,128)(2,1)} %copy-done.2, bf16[18,128,128]{2,1,0:T(8,128)(2,1)} %pad_maximum_fusion.1.win, ...), custom_call_target="tpu_custom_call" | custom-call | tf_op jit(solution)/shard_map/pallas_call | solution.py:119
  78.0 15.1 %all-gather = bf16[1024,128]{1,0:T(8,128)(2,1)} all-gather(bf16[256,128]{1,0:T(8,128)(2,1)} %shard_map.85), channel_id=2, replica_groups=mesh['rows'=128,'feat'=4] {'feat'}, dimensions={0}, use_global_device_ids=true | all-gather | bytes 327680 | tf_op jit(solution)/shard_map/all_gather | solution.py:155
  93.1 3.5 %shard_map.86 = (bf16[256,128]{1,0:T(8,128)(2,1)}, bf16[512,128]{1,0:T(8,128)(2,1)}, f32[2,128,128]{2,1,0:T(8,128)}, bf16[16,128,128]{2,1,0:T(8,128)(2,1)}, f32[2,128,128]{2,1,0:T(8,128)}) custom-call(s32[2]{0:T(128)} %pad_add_fusion.ids, s32[2,8]{1,0:T(2,128)} %columns.3, s32[2]{0:T(128)} %counts.3, bf16[1280,128]{1,0:T(8,128)(2,1)} %copy-done.1, ...), custom_call_target="tpu_custom_call" | custom-call | tf_op jit(solution)/shard_map/pallas_call | solution.py:119
  96.6 11.7 %all_to_all.25 = bf16[16,32,128]{2,1,0:T(8,128)(2,1)S(1)} all-to-all(bf16[16,32,128]{2,1,0:T(8,128)(2,1)} %bitcast.44), channel_id=1, replica_groups={{0,4,8,12,128,132,136,140,256,260,264,268,384,388,392,396},{16,20,24,28..., dimensions={0} | all-to-all | bytes 262144 | tf_op jit(solution)/shard_map/all_to_all | solution.py:181
  108.3 3.5 %all-to-all-start.1 = ((bf16[4,2,256,128]{3,2,1,0:T(8,128)(2,1)}), bf16[4,2,256,128]{3,2,1,0:T(8,128)(2,1)S(1)}, u32[]{:S(2)}, u32[]{:S(2)}) async-start(bf16[4,2,256,128]{3,2,1,0:T(8,128)(2,1)} %bitcast.43), calls=%async_computation.1 | async-start | bytes 1048576 | tf_op jit(solution)/shard_map/all_to_all | solution.py:169
  111.8 8.8 %all-to-all-done.1 = bf16[4,2,256,128]{3,2,1,0:T(8,128)(2,1)S(1)} async-done(((bf16[4,2,256,128]{3,2,1,0:T(8,128)(2,1)}), bf16[4,2,256,128]{3,2,1,0:T(8,128)(2,1)S(1)}, u32[]{:S(2)}, u32[]{:S(2)}) %all-to-all-start.1) | async-done | bytes 524320 | tf_op jit(solution)/shard_map/all_to_all | solution.py:169
  121.3 7.1 %all-to-all-start.3 = ((f32[8,32,128]{2,1,0:T(8,128)}), f32[8,32,128]{2,1,0:T(8,128)S(1)}, u32[]{:S(2)}, u32[]{:S(2)}) async-start(f32[8,32,128]{2,1,0:T(8,128)} %broadcast_in_dim.76), calls=%async_computation.3 | async-start | bytes 262144 | tf_op jit(solution)/shard_map/all_to_all | solution.py:183
  129.5 3.4 %collective-permute-start.5 = (bf16[256,128]{1,0:T(8,128)(2,1)S(1)}, bf16[256,128]{1,0:T(8,128)(2,1)S(1)}, u32[]{:S(2)}, u32[]{:S(2)}) collective-permute-start(bf16[256,128]{1,0:T(8,128)(2,1)S(1)} %broadcast_select_fusion.1), channel_id=1, source_target_pairs={{0,496},{4,500},{8,504},{12,508},{16,32},{20,36},{24,40},{28,44},{... | collective-permute-start | bytes 196616 | tf_op jit(solution)/shard_map/ppermute | solution.py:177
  132.8 9.8 %collective-permute-start.4 = (bf16[256,128]{1,0:T(8,128)(2,1)S(1)}, bf16[256,128]{1,0:T(8,128)(2,1)S(1)}, u32[]{:S(2)}, u32[]{:S(2)}) collective-permute-start(bf16[256,128]{1,0:T(8,128)(2,1)S(1)} %get-tuple-element.16), channel_id=1, source_target_pairs={{0,16},{4,20},{8,24},{12,28},{16,0},{20,4},{24,8},{28,12},{32,48},... | collective-permute-start | bytes 196616 | tf_op jit(solution)/shard_map/ppermute | solution.py:178
  143.4 3.5 %all-to-all-start.4 = ((bf16[16,32,128]{2,1,0:T(8,128)(2,1)}), bf16[16,32,128]{2,1,0:T(8,128)(2,1)S(1)}, u32[]{:S(2)}, u32[]{:S(2)}) async-start(bf16[16,32,128]{2,1,0:T(8,128)(2,1)} %broadcast_in_dim.77), calls=%async_computation.4 | async-start | bytes 262144 | tf_op jit(solution)/shard_map/all_to_all | solution.py:187
  147.6 7.1 %all-to-all-done.4 = bf16[16,32,128]{2,1,0:T(8,128)(2,1)S(1)} async-done(((bf16[16,32,128]{2,1,0:T(8,128)(2,1)}), bf16[16,32,128]{2,1,0:T(8,128)(2,1)S(1)}, u32[]{:S(2)}, u32[]{:S(2)}) %all-to-all-start.4) | async-done | bytes 131104 | tf_op jit(solution)/shard_map/all_to_all | solution.py:187
  154.7 0.7 bitcast_convert_fusion
  (39 shorter events, 3.8 us)
Async XLA Ops:
  0.6 54.7 %copy-start.4 = (bf16[512,128]{1,0:T(8,128)(2,1)S(1)}, bf16[512,128]{1,0:T(8,128)(2,1)}, u32[]{:S(2)}) copy-start(bf16[512,128]{1,0:T(8,128)(2,1)} %param.7) | copy-start | bytes 393220
  0.6 54.7 %copy-start.5 = (bf16[2,2,128,128]{3,2,1,0:T(8,128)(2,1)S(1)}, bf16[2,2,128,128]{3,2,1,0:T(8,128)(2,1)}, u32[]{:S(2)}) copy-start(bf16[2,2,128,128]{3,2,1,0:T(8,128)(2,1)} %param.8) | copy-start | bytes 393220
  0.7 27.0 %collective-permute-start.3 = (bf16[256,128]{1,0:T(8,128)(2,1)}, bf16[256,128]{1,0:T(8,128)(2,1)S(1)}, u32[]{:S(2)}, u32[]{:S(2)}) collective-permute-start(bf16[256,128]{1,0:T(8,128)(2,1)} %param.6), channel_id=1, source_target_pairs={{0,496},{4,500},{8,504},{12,508},{16,32},{20,36},{24,40},{28,44},{... | collective-permute-start | bytes 196616 | tf_op jit(solution)/shard_map/ppermute | solution.py:138
  4.6 23.0 %collective-permute-start.2 = (bf16[256,128]{1,0:T(8,128)(2,1)}, bf16[256,128]{1,0:T(8,128)(2,1)S(1)}, u32[]{:S(2)}, u32[]{:S(2)}) collective-permute-start(bf16[256,128]{1,0:T(8,128)(2,1)} %param.6), channel_id=1, source_target_pairs={{0,16},{4,20},{8,24},{12,28},{16,0},{20,4},{24,8},{28,12},{32,48},... | collective-permute-start | bytes 196616 | tf_op jit(solution)/shard_map/ppermute | solution.py:139
  19.2 39.1 %copy-start.1 = (bf16[1280,128]{1,0:T(8,128)(2,1)}, bf16[1280,128]{1,0:T(8,128)(2,1)S(1)}, u32[]{:S(2)}) copy-start(bf16[1280,128]{1,0:T(8,128)(2,1)S(1)} %pad_maximum_fusion.3.own) | copy-start | bytes 983044
  19.2 39.1 %copy-start.8 = (bf16[256,128]{1,0:T(8,128)(2,1)S(1)}, bf16[256,128]{1,0:T(8,128)(2,1)}, u32[]{:S(2)}) copy-start(bf16[256,128]{1,0:T(8,128)(2,1)} %param.6) | copy-start | bytes 196612
  19.2 36.1 %collective-permute-start = (bf16[1280,128]{1,0:T(8,128)(2,1)S(1)}, bf16[1280,128]{1,0:T(8,128)(2,1)S(1)}, u32[]{:S(2)}, u32[]{:S(2)}) collective-permute-start(bf16[1280,128]{1,0:T(8,128)(2,1)S(1)} %pad_maximum_fusion.3.own), channel_id=1, source_target_pairs={{0,2},{1,3},{2,0},{3,1},{4,6},{5,7},{6,4},{7,5},{8,10},{9,11},{10,... | collective-permute-start | bytes 983048 | tf_op jit(solution)/shard_map/ppermute | solution.py:137
  27.7 46.1 %copy-start.3 = (bf16[256,128]{1,0:T(8,128)(2,1)}, bf16[256,128]{1,0:T(8,128)(2,1)S(1)}, u32[]{:S(2)}) copy-start(bf16[256,128]{1,0:T(8,128)(2,1)S(1)} %get-tuple-element.19.last) | copy-start | bytes 196612
  55.3 3.9 %copy-start = (bf16[1280,128]{1,0:T(8,128)(2,1)}, bf16[1280,128]{1,0:T(8,128)(2,1)S(1)}, u32[]{:S(2)}) copy-start(bf16[1280,128]{1,0:T(8,128)(2,1)S(1)} %collective-permute-done.cross) | copy-start | bytes 983044
  56.2 18.4 %collective-permute-start.1 = (bf16[2560,128]{1,0:T(8,128)(2,1)S(1)}, bf16[2560,128]{1,0:T(8,128)(2,1)S(1)}, u32[]{:S(2)}, u32[]{:S(2)}) collective-permute-start(bf16[2560,128]{1,0:T(8,128)(2,1)S(1)} %pad_maximum_fusion), channel_id=1, source_target_pairs={{0,1},{1,0},{2,3},{3,2},{4,5},{5,4},{6,7},{7,6},{8,9},{9,8},{10,11... | collective-permute-start | bytes 1966088 | tf_op jit(solution)/shard_map/ppermute | solution.py:147
  59.2 14.6 %all-to-all-start = ((bf16[4,2,256,128]{3,2,1,0:T(8,128)(2,1)}), bf16[4,2,256,128]{3,2,1,0:T(8,128)(2,1)S(1)}, u32[]{:S(2)}, u32[]{:S(2)}) async-start(bf16[4,2,256,128]{3,2,1,0:T(8,128)(2,1)} %pad_maximum_fusion.2), calls=%async_computation | async-start | bytes 1048576 | tf_op jit(solution)/shard_map/all_to_all | solution.py:145
  74.7 0.9 copy-start.2
  108.3 12.3 %all-to-all-start.1 = ((bf16[4,2,256,128]{3,2,1,0:T(8,128)(2,1)}), bf16[4,2,256,128]{3,2,1,0:T(8,128)(2,1)S(1)}, u32[]{:S(2)}, u32[]{:S(2)}) async-start(bf16[4,2,256,128]{3,2,1,0:T(8,128)(2,1)} %bitcast.43), calls=%async_computation.1 | async-start | bytes 1048576 | tf_op jit(solution)/shard_map/all_to_all | solution.py:169
  121.3 21.4 %all-to-all-start.3 = ((f32[8,32,128]{2,1,0:T(8,128)}), f32[8,32,128]{2,1,0:T(8,128)S(1)}, u32[]{:S(2)}, u32[]{:S(2)}) async-start(f32[8,32,128]{2,1,0:T(8,128)} %broadcast_in_dim.76), calls=%async_computation.3 | async-start | bytes 262144 | tf_op jit(solution)/shard_map/all_to_all | solution.py:183
  128.5 0.9 copy-start.7
  128.5 18.4 %copy-start.6 = (f32[2,128,128]{2,1,0:T(8,128)S(1)}, f32[2,128,128]{2,1,0:T(8,128)}, u32[]{:S(2)}) copy-start(f32[2,128,128]{2,1,0:T(8,128)} %get-tuple-element.9) | copy-start | bytes 393220
  129.5 17.5 %collective-permute-start.5 = (bf16[256,128]{1,0:T(8,128)(2,1)S(1)}, bf16[256,128]{1,0:T(8,128)(2,1)S(1)}, u32[]{:S(2)}, u32[]{:S(2)}) collective-permute-start(bf16[256,128]{1,0:T(8,128)(2,1)S(1)} %broadcast_select_fusion.1), channel_id=1, source_target_pairs={{0,496},{4,500},{8,504},{12,508},{16,32},{20,36},{24,40},{28,44},{... | collective-permute-start | bytes 196616 | tf_op jit(solution)/shard_map/ppermute | solution.py:177
  132.8 14.1 %collective-permute-start.4 = (bf16[256,128]{1,0:T(8,128)(2,1)S(1)}, bf16[256,128]{1,0:T(8,128)(2,1)S(1)}, u32[]{:S(2)}, u32[]{:S(2)}) collective-permute-start(bf16[256,128]{1,0:T(8,128)(2,1)S(1)} %get-tuple-element.16), channel_id=1, source_target_pairs={{0,16},{4,20},{8,24},{12,28},{16,0},{20,4},{24,8},{28,12},{32,48},... | collective-permute-start | bytes 196616 | tf_op jit(solution)/shard_map/ppermute | solution.py:178
  143.4 11.3 %all-to-all-start.4 = ((bf16[16,32,128]{2,1,0:T(8,128)(2,1)}), bf16[16,32,128]{2,1,0:T(8,128)(2,1)S(1)}, u32[]{:S(2)}, u32[]{:S(2)}) async-start(bf16[16,32,128]{2,1,0:T(8,128)(2,1)} %broadcast_in_dim.77), calls=%async_computation.4 | async-start | bytes 262144 | tf_op jit(solution)/shard_map/all_to_all | solution.py:187
